TPU v7x, 32 devices: a whole 2x2x4 slice. The times are simulated.
32 devices in a mesh: row: 4 (over y, x), col: 8 (over z, core).
Axes of the slice: x: 2, y: 2, z: 4, core: 2. Of those that a mesh axis runs over, the one named last changes fastest.
Arguments:
- gradient: float32 [6144, 12288], P(('row', 'col')), may hold values from -200 to 200
Outputs:
- preconditioned: float32 [6144, 12288], P(('row', 'col'))
All inputs are finite; a program needn't handle non-finite values.
Results may differ from a plain program's by a relative error of at most 0.00023.
Values sent between devices are 32-bit elements; how exact they have to be, the bound alone decides.
A program may use at most 128 MiB of HBM per device.

v0:
```python
import jax
import jax.numpy as jnp
from jax import lax
from jax.sharding import PartitionSpec as P

D = 12288
BLOCK = 768
ITERS = 2


def product(first, second):
    return jnp.matmul(first, second, precision=lax.Precision.HIGHEST)


def inverse_root(gram_matrix):
    matrix_order = gram_matrix.shape[-1]
    identity = jnp.eye(matrix_order, dtype=gram_matrix.dtype)
    norm_scale = jnp.sqrt(jnp.sum(gram_matrix * gram_matrix, axis=(-2, -1), keepdims=True)) + 1e-06
    iterate = gram_matrix / norm_scale
    root_now = identity
    for iteration in range(ITERS):
        factor = (5.0 * identity - iterate) * 0.25
        root_now = factor if iteration == 0 else product(root_now, factor)
        if iteration + 1 < ITERS:
            square = product(factor, factor)
            iterate = product(product(square, square), iterate)
    return root_now * norm_scale ** (-0.25)


def empty_root(gram_matrix):
    return jnp.zeros_like(gram_matrix)


def local(gradient):
    tile_grad = lax.all_to_all(gradient, "col", split_axis=1, concat_axis=0, tiled=True)
    row_blocks = tile_grad.shape[0] // BLOCK
    col_blocks = tile_grad.shape[1] // BLOCK
    blocks = tile_grad.reshape(row_blocks, BLOCK, col_blocks, BLOCK)
    left_part = jnp.einsum("aibj,akbj->aik", blocks, blocks, precision=lax.Precision.HIGHEST) / D
    right_part = jnp.einsum("aibj,aibk->bjk", blocks, blocks, precision=lax.Precision.HIGHEST) / D
    left_gram = lax.psum(left_part, "col")
    right_gram = lax.psum(right_part, "row")
    row_here = lax.axis_index("row")
    col_here = lax.axis_index("col")
    row_total = lax.axis_size("row")
    col_total = lax.axis_size("col")
    left_owners = []
    left_owned = []
    for block_row in range(row_blocks):
        owner_col = (row_here + 1 + block_row) % col_total
        left_owners.append(owner_col)
        left_owned.append(
            lax.cond(col_here == owner_col, inverse_root, empty_root, left_gram[block_row])
        )
    right_owners = []
    right_owned = []
    for block_col in range(col_blocks):
        owner_row = (col_here * col_blocks + block_col) % row_total
        right_owners.append(owner_row)
        right_owned.append(
            lax.cond(row_here == owner_row, inverse_root, empty_root, right_gram[block_col])
        )
    left_roots = lax.psum(jnp.stack(left_owned), "col")
    right_roots = lax.psum(jnp.stack(right_owned), "row")
    mixed_rows = jnp.einsum("aik,akbj->aibj", left_roots, blocks, precision=lax.Precision.HIGHEST)
    result = jnp.einsum("aibj,bjl->aibl", mixed_rows, right_roots, precision=lax.Precision.HIGHEST)
    tile_out = result.reshape(tile_grad.shape[0], tile_grad.shape[1])
    return lax.all_to_all(tile_out, "col", split_axis=0, concat_axis=1, tiled=True)


def solution(mesh):
    in_specs = (P(("row", "col"), None),)
    out_specs = P(("row", "col"), None)
    return jax.shard_map(local, mesh=mesh, in_specs=in_specs, out_specs=out_specs, check_vma=False)
```

profile of v0, /device:TPU:0, one launch (start us, length us, event | category | flops | bytes accessed | tf_op | source)
XLA Modules:
  0.0 988.0 jit_solution(14985175931717549455)
XLA Ops:
  6.5 4.5 copy.45
  11.1 212.6 %all_to_all.35 = f32[192,8,1536]{2,0,1:T(8,128)} all-to-all(f32[192,8,1536]{2,0,1:T(8,128)S(1)} %bitcast.97), channel_id=1, replica_groups=mesh['row'=4,'col'=8] {'col'}, dimensions={1} | all-to-all | bytes 18874368 | tf_op jit(solution)/shard_map/all_to_all | solution.py:35
  223.7 12.1 %reshape.108 = f32[2,768,2,768]{3,2,1,0:T(2,128)} reshape(f32[8,192,1536]{2,1,0:T(8,128)} %bitcast.95) | data formatting | bytes 18874368 | tf_op jit(solution)/shard_map/reshape | solution.py:38
  235.7 29.4 %bitcast_multiply_fusion = f32[2,768,768]{2,1,0:T(8,128)} fusion(f32[2,768,2,768]{3,2,1,0:T(2,128)} %reshape.108), kind=kOutput, calls=%fused_computation.132 | convolution fusion | flops 21744451584 | bytes 14155776 | tf_op jit(solution)/shard_map/aibj,akbj->aik/dot_general | solution.py:39
  265.1 0.6 all-reduce.5.cloned.1.call-start
  265.7 35.0 %bitcast_multiply_fusion.1 = f32[2,768,768]{2,1,0:T(8,128)} fusion(f32[2,768,2,768]{3,2,1,0:T(2,128)} %reshape.108), kind=kOutput, calls=%fused_computation.133 | convolution fusion | flops 21744451584 | bytes 14155776 | tf_op jit(solution)/shard_map/aibj,aibk->bjk/dot_general | solution.py:40
  300.7 0.0 all-reduce.11.cloned.1.call-start
  300.8 69.8 %all-reduce.9.cloned.1.call-done = f32[2,768,768]{2,1,0:T(8,128)} async-done(((f32[2,768,768]{2,1,0:T(8,128)}), f32[2,768,768]{2,1,0:T(8,128)}) %all-reduce.9.cloned.1.call-update) | async-done | bytes 4718608 | tf_op jit(solution)/shard_map/psum | solution.py:41
  370.6 8.9 conditional.7
  370.6 0.2 stack.30
  379.5 14.3 %conditional.6 = (f32[1,768,768]{2,1,0:T(8,128)}) conditional(s32[]{:T(128)} %convert_element_type.18, () %tuple.39, f32[2,768,768]{2,1,0:T(8,128)} %all-reduce.9.cloned.1.call-done), branch_computations={%region_9.10_spmd, %region_10.0_spmd} | conditional | flops 21753888768 | bytes 44826712 | solution.py:53
  379.5 1.7 stack.28
  393.8 4.1 pad_maximum_fusion.1
  398.1 88.2 %all-reduce.5.cloned.1.call-done = f32[2,768,768]{2,1,0:T(8,128)} async-done(((f32[2,768,768]{2,1,0:T(8,128)}), f32[2,768,768]{2,1,0:T(8,128)}) %all-reduce.5.cloned.1.call-update) | async-done | bytes 4718608 | tf_op jit(solution)/shard_map/psum | solution.py:42
  486.2 9.1 conditional.5
  486.2 0.2 stack.26.clone
  495.3 39.0 %conditional.4 = (f32[1,768,768]{1,2,0:T(8,128)}) conditional(s32[]{:T(128)} %convert_element_type.16, () %tuple.37, f32[2,768,768]{2,1,0:T(8,128)} %all-reduce.5.cloned.1.call-done), branch_computations={%region_1.0_spmd, %region_2.4_spmd} | conditional | flops 21753888768 | bytes 49545304 | solution.py:61
  495.4 2.9 multiply_reduce_fusion
  499.0 8.7 fusion.5
  507.7 6.0 fusion.132
  513.6 7.4 fusion.7
  521.1 9.9 %multiply_bitcast_fusion = f32[1,768,768]{2,1,0:T(8,128)} fusion(f32[768,768]{1,0:T(8,128)} %fusion.7, f32[]{:T(128)S(6)} %pow.12, f32[2,768,768]{2,1,0:T(8,128)} %param.1, f32[]{:T(128)S(6)} %add.38), kind=kOutput, calls=%fused_computation.10 | convolution fusion | flops 5441716224 | bytes 7077896 | tf_op jit(solution)/shard_map/cond/branch_1_fun/dot_general | solution.py:12
  531.0 3.1 copy.29
  534.3 4.1 pad_maximum_fusion
  538.4 56.6 %all-reduce.11.cloned.1.call-done = f32[2,768,768]{2,1,0:T(8,128)} async-done(((f32[2,768,768]{2,1,0:T(8,128)}), f32[2,768,768]{2,1,0:T(8,128)}) %all-reduce.11.cloned.1.call-update) | async-done | bytes 4718608 | tf_op jit(solution)/shard_map/psum | solution.py:63
  595.0 28.1 %fusion.118 = f32[2,768,2,768]{3,1,0,2:T(8,128)} fusion(f32[2,768,2,768]{3,2,1,0:T(2,128)} %reshape.108, f32[2,768,768]{2,1,0:T(8,128)} %all-reduce.11.cloned.1.call-done), kind=kOutput, calls=%fused_computation.123 | convolution fusion | flops 21743271936 | bytes 23592960 | tf_op jit(solution)/shard_map/aik,akbj->aibj/dot_general | solution.py:65
  623.1 87.4 %all-reduce.7.cloned.1.call-done = f32[2,768,768]{1,2,0:T(8,128)} async-done(((f32[2,768,768]{1,2,0:T(8,128)}), f32[2,768,768]{1,2,0:T(8,128)}) %all-reduce.7.cloned.1.call-update) | async-done | bytes 4718608 | tf_op jit(solution)/shard_map/psum | solution.py:64
  710.5 27.2 %fusion.125 = f32[2,768,2,768]{1,3,0,2:T(8,128)} fusion(f32[2,768,2,768]{3,1,0,2:T(8,128)} %fusion.118, f32[2,768,768]{1,2,0:T(8,128)} %all-reduce.7.cloned.1.call-done), kind=kOutput, calls=%fused_computation.134 | convolution fusion | flops 21743271936 | bytes 23592960 | tf_op jit(solution)/shard_map/aibj,bjl->aibl/dot_general | solution.py:66
  737.7 14.9 %copy.23 = f32[2,768,2,768]{3,2,1,0:T(2,128)} copy(f32[2,768,2,768]{1,3,0,2:T(8,128)} %fusion.125) | data formatting | bytes 18874368 | tf_op jit(solution)/shard_map/aibj,bjl->aibl/transpose | solution.py:66
  752.6 13.1 %all_to_all.29 = f32[8,192,1536]{2,1,0:T(8,128)} reshape(f32[2,768,2,768]{3,2,1,0:T(2,128)} %copy.23) | data formatting | bytes 18874368 | tf_op jit(solution)/shard_map/all_to_all | solution.py:68
  765.6 210.9 %all_to_all.36 = f32[8,192,1536]{2,1,0:T(8,128)S(1)} all-to-all(f32[8,192,1536]{2,1,0:T(8,128)} %all_to_all.29), channel_id=1, replica_groups=mesh['row'=4,'col'=8] {'col'}, dimensions={0} | all-to-all | bytes 18874368 | tf_op jit(solution)/shard_map/all_to_all | solution.py:68
  976.6 4.6 copy.33
  (8 shorter events, 0.1 us)
Async XLA Ops:
  6.5 364.1 %all-reduce.9.cloned.1.call-start = ((), (), s32[]{:S(2)}) async-start(), calls=%async_computation.4 | async-start | bytes 9437184 | tf_op jit(solution)/shard_map/psum | solution.py:41
  265.1 221.1 %all-reduce.5.cloned.1.call-start = ((), (), s32[]{:S(2)}) async-start(), calls=%async_computation.2 | async-start | bytes 9437184 | tf_op jit(solution)/shard_map/psum | solution.py:42
  300.7 294.3 %all-reduce.11.cloned.1.call-start = ((), (), s32[]{:S(2)}) async-start(), calls=%async_computation.5 | async-start | bytes 9437184 | tf_op jit(solution)/shard_map/psum | solution.py:63
  398.0 312.5 %all-reduce.7.cloned.1.call-start = ((), (), s32[]{:S(2)}) async-start(), calls=%async_computation.3 | async-start | bytes 9437184 | tf_op jit(solution)/shard_map/psum | solution.py:64
  507.6 6.0 copy-start
Sparse Core Ops, SparseCore 0:
  265.3 105.2 all-reduce.8
  373.9 112.3 all-reduce.4
  488.6 106.3 all-reduce.10
  598.1 112.3 all-reduce.6
where the time goes:
time: 994 us; the launch traced here: 988 us
  blocking collectives  424 us (43%)
  waiting for transfers between devices  302 us (30%)
  matrix products  152 us (15%)
  local copies, waits for them, and re-layouts  54.1 us (5%)
  loops' own time  31.3 us (3%)
  between operations  13.5 us (1%)
  other arithmetic  11.2 us (1%)
    all_to_all x1, blocking collectives, local(): lax.all_to_all(gradient, 'col', split_axis=1, concat_axis=0, tiled=True)  213 us
    all_to_all x1, blocking collectives, local(): lax.all_to_all(tile_out, 'col', split_axis=0, concat_axis=1, tiled=True)  211 us
    psum x1, waiting for transfers between devices, local(): right_gram = lax.psum(right_part, 'row')  88.2 us
    psum x1, waiting for transfers between devices, local(): right_roots = lax.psum(jnp.stack(right_owned), 'row')  87.4 us
    psum x1, waiting for transfers between devices, local(): left_gram = lax.psum(left_part, 'col')  69.8 us
    psum x1, waiting for transfers between devices, local(): left_roots = lax.psum(jnp.stack(left_owned), 'col')  56.6 us
    dot_general x1, matrix products, local(): jnp.einsum('aibj,aibk->bjk', blocks, blocks, precision=lax.Precision.HIGH...  35 us
    dot_general x4, matrix products, product(): return jnp.matmul(first, second, precision=lax.Precision.HIGHEST)  32 us
  transfers between devices with their start and end apart: 4, of which 4 were waited for; matrix products, arithmetic and copies ran while one was open for 11% of the time, Pallas kernels for 0%

commit v1 on v0

--- a/solution.py
+++ b/solution.py
@@ -6,6 +6,15 @@
 D = 12288
 BLOCK = 768
 ITERS = 2
+
+
+def rest_goods_now(device_axis, s0):
+    world = lax.axis_size(device_axis)
+    v_now = lambda mid_arr: [(idx, idx ^ mid_arr) for idx in range(world)]
+    e_next = s0
+    for dev_j in range(world.bit_length() - 1):
+        e_next = e_next + lax.ppermute(e_next, axis_name=device_axis, perm=v_now(1 << dev_j))
+    return e_next
 
 
 def product(first, second):
@@ -38,7 +47,7 @@
     blocks = tile_grad.reshape(row_blocks, BLOCK, col_blocks, BLOCK)
     left_part = jnp.einsum("aibj,akbj->aik", blocks, blocks, precision=lax.Precision.HIGHEST) / D
     right_part = jnp.einsum("aibj,aibk->bjk", blocks, blocks, precision=lax.Precision.HIGHEST) / D
-    left_gram = lax.psum(left_part, "col")
+    left_gram = rest_goods_now("col", s0=left_part)
     right_gram = lax.psum(right_part, "row")
     row_here = lax.axis_index("row")
     col_here = lax.axis_index("col")

time: 994 us -> 1150 us (1.16)
  waiting for transfers between devices: 302 us -> 447 us
    ppermute x0 -> x3, waiting for transfers between devices: none -> 276 us  [rest_goods_now(): lax.ppermute(e_next, axis_name=device_axis, perm=v_now(1 << dev_j))]
    psum x1, waiting for transfers between devices: 88.2 us -> 0.02 us  [local(): right_gram = lax.psum(right_part, 'row')]
    psum x1 -> x0, waiting for transfers between devices: 69.8 us -> none  [local(): left_gram = lax.psum(left_part, 'col')]
    psum x1, waiting for transfers between devices: 56.6 us -> 84.1 us  [local(): left_roots = lax.psum(jnp.stack(left_owned), 'col')]
  transfers between devices with their start and end apart: 4 -> 6, of which waited for: 4 -> 5; matrix products, arithmetic and copies ran while one was open for 11% -> 11% of each run, Pallas kernels for 0% -> 0%
where the time goes in v1:
time: 1150 us; the launch traced here: 1140 us
  waiting for transfers between devices  447 us (39%)
  blocking collectives  424 us (37%)
  matrix products  157 us (14%)
  local copies, waits for them, and re-layouts  54.1 us (5%)
  loops' own time  24 us (2%)
  other arithmetic  21.1 us (2%)
  between operations  13.8 us (1%)
    ppermute x3, waiting for transfers between devices, rest_goods_now(): lax.ppermute(e_next, axis_name=device_axis, perm=v_now(1 << dev_j))  276 us
    all_to_all x1, blocking collectives, local(): lax.all_to_all(gradient, 'col', split_axis=1, concat_axis=0, tiled=True)  213 us
    all_to_all x1, blocking collectives, local(): lax.all_to_all(tile_out, 'col', split_axis=0, concat_axis=1, tiled=True)  211 us
    psum x1, waiting for transfers between devices, local(): right_roots = lax.psum(jnp.stack(right_owned), 'row')  87.5 us
    psum x1, waiting for transfers between devices, local(): left_roots = lax.psum(jnp.stack(left_owned), 'col')  84.1 us
    dot_general x1, matrix products, local(): jnp.einsum('aibj,aibk->bjk', blocks, blocks, precision=lax.Precision.HIGH...  41 us
    dot_general x4, matrix products, product(): return jnp.matmul(first, second, precision=lax.Precision.HIGHEST)  32.4 us
    dot_general x1, matrix products, local(): jnp.einsum('aik,akbj->aibj', left_roots, blocks, precision=lax.Precision....  28.1 us
  transfers between devices with their start and end apart: 6, of which 5 were waited for; matrix products, arithmetic and copies ran while one was open for 11% of the time, Pallas kernels for 0%

profile of v1, /device:TPU:0, one launch (start us, length us, event | category | flops | bytes accessed | tf_op | source)
XLA Modules:
  0.0 1140.9 jit_solution(9208639304234540513)
XLA Ops:
  6.5 4.5 copy.45
  11.1 212.6 %all_to_all.35 = f32[192,8,1536]{2,0,1:T(8,128)} all-to-all(f32[192,8,1536]{2,0,1:T(8,128)S(1)} %bitcast.97), channel_id=1, replica_groups=mesh['row'=4,'col'=8] {'col'}, dimensions={1} | all-to-all | bytes 18874368 | tf_op jit(solution)/shard_map/all_to_all | solution.py:44
  223.7 12.1 %reshape.108 = f32[2,768,2,768]{3,2,1,0:T(2,128)} reshape(f32[8,192,1536]{2,1,0:T(8,128)} %bitcast.95) | data formatting | bytes 18874368 | tf_op jit(solution)/shard_map/reshape | solution.py:47
  235.7 27.9 %bitcast_multiply_fusion = f32[2,768,768]{2,1,0:T(8,128)S(1)} fusion(f32[2,768,2,768]{3,2,1,0:T(2,128)} %reshape.108), kind=kOutput, calls=%fused_computation.132 | convolution fusion | flops 21744451584 | bytes 14155776 | tf_op jit(solution)/shard_map/aibj,akbj->aik/dot_general | solution.py:48
  263.7 7.9 collective-permute-done
  271.6 0.6 add.63
  272.3 103.8 %collective-permute-done.1 = f32[2,768,768]{2,1,0:T(8,128)S(1)} collective-permute-done((f32[2,768,768]{2,1,0:T(8,128)S(1)}, f32[2,768,768]{2,1,0:T(8,128)S(1)}, u32[]{:S(2)}, u32[]{:S(2)}) %collective-permute-start.1) | collective-permute-done | bytes 4718624 | tf_op jit(solution)/shard_map/ppermute | solution.py:16
  376.1 2.8 add.64
  379.0 41.0 %bitcast_multiply_fusion.1 = f32[2,768,768]{2,1,0:T(8,128)} fusion(f32[2,768,2,768]{3,2,1,0:T(2,128)S(1)} %bitcast.99), kind=kOutput, calls=%fused_computation.133 | convolution fusion | flops 21744451584 | bytes 14155776 | tf_op jit(solution)/shard_map/aibj,aibk->bjk/dot_general | solution.py:49
  420.1 164.1 %collective-permute-done.2 = f32[2,768,768]{2,1,0:T(8,128)} collective-permute-done((f32[2,768,768]{2,1,0:T(8,128)}, f32[2,768,768]{2,1,0:T(8,128)}, u32[]{:S(2)}, u32[]{:S(2)}) %collective-permute-start.2) | collective-permute-done | bytes 4718624 | tf_op jit(solution)/shard_map/ppermute | solution.py:16
  584.2 6.6 add.65
  590.8 0.6 conditional.6
  591.4 14.2 %conditional.7 = (f32[1,768,768]{2,1,0:T(8,128)}) conditional(s32[]{:T(128)} %convert_element_type.19, () %tuple.40, f32[2,768,768]{2,1,0:T(8,128)} %add.65), branch_computations={%region_11.12_spmd, %region_12.0_spmd} | conditional | flops 21753888768 | bytes 40108140 | solution.py:62
  591.4 1.5 stack.30
  605.5 4.1 pad_maximum_fusion.1
  609.8 10.1 conditional.5
  619.8 39.5 %conditional.4 = (f32[1,768,768]{1,2,0:T(8,128)}) conditional(s32[]{:T(128)} %convert_element_type.16, () %tuple.37, f32[2,768,768]{2,1,0:T(8,128)} %all-reduce.4.cloned.1.call-done), branch_computations={%region_1.2_spmd, %region_2.4_spmd} | conditional | flops 21753888768 | bytes 49545304 | solution.py:70
  619.9 2.9 multiply_reduce_fusion
  623.5 8.6 fusion.5
  632.1 6.0 fusion.132
  638.1 7.5 fusion.7
  645.7 10.3 multiply_bitcast_fusion
  655.9 3.1 copy.29
  659.3 4.1 pad_maximum_fusion
  663.4 84.1 %all-reduce.8.cloned.1.call-done = f32[2,768,768]{2,1,0:T(8,128)} async-done(((f32[2,768,768]{2,1,0:T(8,128)}), f32[2,768,768]{2,1,0:T(8,128)}) %all-reduce.8.cloned.1.call-update) | async-done | bytes 4718608 | tf_op jit(solution)/shard_map/psum | solution.py:72
  747.5 28.1 %fusion.118 = f32[2,768,2,768]{3,1,0,2:T(8,128)} fusion(f32[2,768,2,768]{3,2,1,0:T(2,128)} %reshape.108, f32[2,768,768]{2,1,0:T(8,128)} %all-reduce.8.cloned.1.call-done), kind=kOutput, calls=%fused_computation.123 | convolution fusion | flops 21743271936 | bytes 23592960 | tf_op jit(solution)/shard_map/aik,akbj->aibj/dot_general | solution.py:74
  775.6 87.5 %all-reduce.6.cloned.1.call-done = f32[2,768,768]{1,2,0:T(8,128)} async-done(((f32[2,768,768]{1,2,0:T(8,128)}), f32[2,768,768]{1,2,0:T(8,128)}) %all-reduce.6.cloned.1.call-update) | async-done | bytes 4718608 | tf_op jit(solution)/shard_map/psum | solution.py:73
  863.1 27.2 %fusion.125 = f32[2,768,2,768]{1,3,0,2:T(8,128)} fusion(f32[2,768,2,768]{3,1,0,2:T(8,128)} %fusion.118, f32[2,768,768]{1,2,0:T(8,128)} %all-reduce.6.cloned.1.call-done), kind=kOutput, calls=%fused_computation.134 | convolution fusion | flops 21743271936 | bytes 23592960 | tf_op jit(solution)/shard_map/aibj,bjl->aibl/dot_general | solution.py:75
  890.4 14.9 %copy.23 = f32[2,768,2,768]{3,2,1,0:T(2,128)} copy(f32[2,768,2,768]{1,3,0,2:T(8,128)} %fusion.125) | data formatting | bytes 18874368 | tf_op jit(solution)/shard_map/aibj,bjl->aibl/transpose | solution.py:75
  905.3 13.1 %all_to_all.29 = f32[8,192,1536]{2,1,0:T(8,128)} reshape(f32[2,768,2,768]{3,2,1,0:T(2,128)} %copy.23) | data formatting | bytes 18874368 | tf_op jit(solution)/shard_map/all_to_all | solution.py:77
  918.4 210.9 %all_to_all.36 = f32[8,192,1536]{2,1,0:T(8,128)S(1)} all-to-all(f32[8,192,1536]{2,1,0:T(8,128)} %all_to_all.29), channel_id=1, replica_groups=mesh['row'=4,'col'=8] {'col'}, dimensions={0} | all-to-all | bytes 18874368 | tf_op jit(solution)/shard_map/all_to_all | solution.py:77
  1129.3 4.6 copy.33
  (21 shorter events, 0.7 us)
Async XLA Ops:
  6.5 603.2 %all-reduce.4.cloned.1.call-start = ((), (), s32[]{:S(2)}) async-start(), calls=%async_computation.2 | async-start | bytes 9437184 | tf_op jit(solution)/shard_map/psum | solution.py:51
  263.6 8.0 collective-permute-start
  271.6 107.5 %slice-start = ((s8[9437184]{0:T(1024)(128)(4,1)}), s8[4194304]{0:T(1024)(128)(4,1)S(1)}, s32[]{:S(2)}) async-start(s8[9437184]{0:T(1024)(128)(4,1)} %bitcast.98), calls=%async_computation.5 | async-start | bytes 8388608
  271.6 107.5 %slice-start.1 = ((s8[9437184]{0:T(1024)(128)(4,1)}), s8[4194304]{0:T(1024)(128)(4,1)S(1)}, s32[]{:S(2)}) async-start(s8[9437184]{0:T(1024)(128)(4,1)} %bitcast.98), calls=%async_computation.6 | async-start | bytes 8388608
  272.2 106.8 %slice-start.2 = ((s8[9437184]{0:T(1024)(128)(4,1)}), s8[1048576]{0:T(1024)(128)(4,1)S(1)}, s32[]{:S(2)}) async-start(s8[9437184]{0:T(1024)(128)(4,1)} %bitcast.98), calls=%async_computation.7 | async-start | bytes 2097152
  272.2 103.9 %collective-permute-start.1 = (f32[2,768,768]{2,1,0:T(8,128)S(1)}, f32[2,768,768]{2,1,0:T(8,128)S(1)}, u32[]{:S(2)}, u32[]{:S(2)}) collective-permute-start(f32[2,768,768]{2,1,0:T(8,128)S(1)} %add.63), channel_id=1, source_target_pairs={{0,2},{1,3},{2,0},{3,1},{4,6},{5,7},{6,4},{7,5},{8,10},{9,11},{10,... | collective-permute-start | bytes 14155784 | tf_op jit(solution)/shard_map/ppermute | solution.py:16
  378.9 205.3 %collective-permute-start.2 = (f32[2,768,768]{2,1,0:T(8,128)}, f32[2,768,768]{2,1,0:T(8,128)}, u32[]{:S(2)}, u32[]{:S(2)}) collective-permute-start(f32[2,768,768]{2,1,0:T(8,128)} %add.64), channel_id=1, source_target_pairs={{0,4},{1,5},{2,6},{3,7},{4,0},{5,1},{6,2},{7,3},{8,12},{9,13},{10,... | collective-permute-start | bytes 14155784 | tf_op jit(solution)/shard_map/ppermute | solution.py:16
  420.0 327.5 %all-reduce.8.cloned.1.call-start = ((), (), s32[]{:S(2)}) async-start(), calls=%async_computation.4 | async-start | bytes 9437184 | tf_op jit(solution)/shard_map/psum | solution.py:72
  609.7 253.5 %all-reduce.6.cloned.1.call-start = ((), (), s32[]{:S(2)}) async-start(), calls=%async_computation.3 | async-start | bytes 9437184 | tf_op jit(solution)/shard_map/psum | solution.py:73
  632.1 6.0 copy-start
Sparse Core Ops, SparseCore 0:
  420.1 112.7 all-reduce.3
  609.8 137.6 all-reduce.7
  750.8 112.3 all-reduce.5
